TPU v7x, 512 devices: a whole 4x4x16 slice. The times are simulated.
512 devices in a mesh: rows: 64 (over y, z_lo, core), feat: 8 (over x, z_hi).
Axes of the slice: x: 4, y: 4, z: 16 (z_hi: 2, z_lo: 8; z = z_hi * 8 + z_lo), core: 2. Of those that a mesh axis runs over, the one named last changes fastest.
Arguments:
- logits: float32 [196608, 32], P('rows'), may hold values from -6 to 6
- labels: int32 [196608], P('rows'), may hold values from 0 to 31
- node_ids: int32 [196608], P('rows'), may hold values from 0 to 7
- bin_codes: int32 [196608, 256], P('rows', 'feat'), may hold values from 0 to 63
- split_feature: int32 [8], replicated, may hold values from 0 to 255
- split_bin: int32 [8], replicated, may hold values from 1 to 63
- split_missing: int32 [8], replicated, may hold values from 0 to 1
Outputs:
- new_logits: float32 [196608, 32], P('rows')
- gain_table: float32 [64, 32, 128], P('rows', 'feat')
- leaves: float32 [8, 2, 32], replicated
Inputs may be any that keep to these rules, and one draw needn't show every extreme that they name: `split_missing`: 1 sends the missing code 64 - 1 to the left child, 0 to the right child.
All inputs are finite; a program needn't handle non-finite values.
Results may differ from a plain program's by a relative error of at most 0.0014.
Values sent between devices are 32-bit elements; how exact they have to be, the bound alone decides.
A program may use at most 64 MiB of HBM per device.

v0:
```python
import math
import jax
import jax.numpy as jnp
from jax import lax
from jax.sharding import PartitionSpec as P

BINS = 64
reg_lambda = 1.0
step_size = 0.3


def split_score(sums, classes):
    grad_part = sums[..., :classes]
    hess_part = sums[..., classes:]
    return jnp.sum(grad_part * grad_part / (hess_part + reg_lambda), axis=-1)


def local(logits, labels, node_ids, bin_codes, split_feature, split_bin, split_missing):
    rows_dev, classes = logits.shape
    feats_dev = bin_codes.shape[1]
    node_count = split_feature.shape[0]
    bin_count = BINS
    per_node = lax.axis_size("rows") // node_count
    pairs_dev = feats_dev // per_node
    feat_pairs = feats_dev // 2
    width = 2 * classes
    expo_vals = jnp.exp(logits)
    soft_prob = expo_vals / jnp.sum(expo_vals, axis=1, keepdims=True)
    class_iota = jnp.arange(classes, dtype=jnp.int32)
    target = (labels[:, None] == class_iota[None, :]).astype(jnp.float32)
    grad_hess = jnp.concatenate(
        [
            (soft_prob - target).astype(jnp.bfloat16),
            (soft_prob * (1.0 - soft_prob)).astype(jnp.bfloat16),
        ],
        axis=1,
    )
    node_iota = jnp.arange(node_count, dtype=jnp.int32)
    node_match = node_ids[:, None] == node_iota[None, :]
    masked_rows = jnp.where(
        node_match[:, :, None], grad_hess[:, None, :], jnp.zeros((), jnp.bfloat16)
    ).reshape(rows_dev, node_count * width)
    bin_iota = jnp.arange(bin_count, dtype=jnp.int32)
    feat_block = math.gcd(feats_dev, 8)
    block_count = feats_dev // feat_block

    def make_hot(codes):
        return (
            (codes[:, :, None] == bin_iota[None, None, :])
            .astype(jnp.bfloat16)
            .reshape(rows_dev, codes.shape[1] * bin_count)
        )

    own_rows = node_count * feat_pairs * width // lax.axis_size("rows")
    groups = lax.axis_size("rows") * own_rows // width
    node_span = groups // feat_pairs

    def block_product(block):
        block_codes = lax.dynamic_slice_in_dim(bin_codes, block * feat_block, feat_block, 1)
        return lax.dot_general(
            masked_rows,
            make_hot(block_codes),
            (((0,), (0,)), ((), ())),
            preferred_element_type=jnp.float32,
        )

    stacked = lax.map(block_product, jnp.arange(block_count, dtype=jnp.int32))
    product = stacked.transpose(1, 0, 2).reshape(node_span * width, feats_dev * bin_count)
    product = product.reshape(node_span, width, feat_pairs, 2 * bin_count).transpose(0, 2, 1, 3)
    owned_hist = lax.psum_scatter(
        product.reshape(lax.axis_size("rows") * own_rows, 2 * bin_count),
        "rows",
        scatter_dimension=0,
        tiled=True,
    )
    owned = (
        owned_hist.reshape(pairs_dev // 2, width, 2, bin_count)
        .transpose(0, 2, 3, 1)
        .reshape(pairs_dev, bin_count, width)
    )
    lower_mask = (
        (bin_iota[:, None] < bin_iota[None, :]) & (bin_iota[:, None] < bin_count - 1)
    ).astype(jnp.float32)
    left_base = jnp.einsum("pbc,bt->ptc", owned, lower_mask, precision=lax.Precision.HIGHEST)
    node_total = jnp.sum(owned, axis=1, keepdims=True)
    missing_sum = owned[:, bin_count - 1 :, :]
    left_miss = left_base + missing_sum
    parent_score = split_score(node_total, classes)
    gain_left = (
        split_score(left_miss, classes)
        + split_score(node_total - left_miss, classes)
        - parent_score
    )
    gain_right = (
        split_score(left_base, classes)
        + split_score(node_total - left_base, classes)
        - parent_score
    )
    gain_rows = (jnp.concatenate([gain_left, gain_right], axis=1) / (2.0 * classes))[None]
    row_feature = jnp.sum(jnp.where(node_match, split_feature[None, :], 0), axis=1)
    row_bin = jnp.sum(jnp.where(node_match, split_bin[None, :], 0), axis=1)
    row_missing = jnp.sum(jnp.where(node_match, split_missing[None, :], 0), axis=1)
    feat_index = lax.axis_index("feat")
    local_col = row_feature - feat_index * feats_dev
    is_owned = (local_col >= 0) & (local_col < feats_dev)
    col_iota = jnp.arange(feats_dev, dtype=jnp.int32)
    row_code = jnp.sum(jnp.where(col_iota[None, :] == local_col[:, None], bin_codes, 0), axis=1)
    goes_left = (row_code < row_bin) | (row_code == bin_count - 1) & (row_missing == 1)
    right_flag = jnp.where(is_owned & jnp.logical_not(goes_left), 1.0, 0.0).astype(jnp.float32)
    side_count = lax.psum(right_flag, "feat")
    row_side = (side_count > 0.5).astype(jnp.int32)
    slot_iota = jnp.arange(2 * node_count, dtype=jnp.int32)
    slot_hot = (node_ids * 2 + row_side)[:, None] == slot_iota[None, :]
    row_index = lax.axis_index("rows")
    my_node = row_index // per_node
    base_feat = feat_index * feats_dev + row_index % per_node * pairs_dev
    local_feat = split_feature[my_node] - base_feat
    holds = ((local_feat >= 0) & (local_feat < pairs_dev)).astype(jnp.float32)
    chosen = owned[jnp.clip(local_feat, 0, pairs_dev - 1)]
    bin_mask = ((bin_iota < split_bin[my_node]) & (bin_iota < bin_count - 1)).astype(jnp.float32)
    left_sum = jnp.sum(chosen * bin_mask[:, None], axis=0) + chosen[bin_count - 1] * split_missing[
        my_node
    ].astype(jnp.float32)
    node_sum = jnp.sum(chosen, axis=0)
    entry = jnp.stack([left_sum, node_sum - left_sum], axis=0) * holds
    placed = jnp.where(
        (node_iota == my_node)[:, None, None], entry[None], jnp.zeros((), jnp.float32)
    )
    side_sums = lax.psum(placed, ("rows", "feat"))
    leaves = -side_sums[..., :classes] / (side_sums[..., classes:] + reg_lambda)
    update = jnp.dot(
        slot_hot.astype(jnp.float32),
        leaves.reshape(2 * node_count, classes),
        precision=lax.Precision.HIGHEST,
    )
    new_logits = logits + step_size * update
    return (new_logits, gain_rows, leaves)


def solution(mesh):
    return jax.shard_map(
        local,
        mesh=mesh,
        in_specs=(P("rows", None), P("rows"), P("rows"), P("rows", "feat"), P(), P(), P()),
        out_specs=(P("rows", None), P("rows", "feat", None), P()),
        check_vma=False,
    )
```

profile of v0, /device:TPU:1, one launch (start us, length us, event | category | flops | bytes accessed | tf_op | source)
XLA Modules:
  0.0 613.6 jit_solution(12515425515692365684)
XLA Ops:
  7.2 1.1 exponential_reduce_fusion
  8.3 0.7 iota_compare_fusion.4
  9.0 1.1 subtract_convert_fusion
  10.2 25.2 %while.11 = (s32[]{:T(128)}, f32[4,512,512]{1,2,0:T(8,128)}, s32[4]{0:T(128)S(1)}, s32[3072,32]{0,1:T(8,128)}, bf16[3072,64]{0,1:T(8,128)(2,1)S(1)}, /*index=5*/...) while((s32[]{:T(128)}, f32[4,512,512]{1,2,0:T(8,128)}, ...), condition=%wide.region_7.8_spmd.clone, body=%wide.region_6.7_spmd.clone.sunk | while | flops 1613758464 | bytes 11207331 | solution.py:67
  10.2 0.6 dynamic_slice.31
  11.5 0.9 constant_dynamic-slice_fusion.2
  12.4 0.9 bitcast_compare_fusion.2
  13.7 2.8 fusion.35
  17.7 0.9 constant_dynamic-slice_fusion.2
  18.7 0.9 bitcast_compare_fusion.2
  19.9 2.8 fusion.35
  22.8 0.6 dynamic_slice.31
  24.0 0.9 constant_dynamic-slice_fusion.2
  25.0 0.9 bitcast_compare_fusion.2
  26.3 2.8 fusion.35
  29.1 0.6 dynamic_slice.31
  30.3 0.9 constant_dynamic-slice_fusion.2
  31.3 0.9 bitcast_compare_fusion.2
  32.5 2.8 fusion.35
  35.4 5.4 copy.31
  40.8 5.5 reshape_reshape.3
  46.3 5.4 copy.32
  52.3 0.6 dynamic_slice.19
  53.5 0.6 dynamic_slice.21
  54.1 0.6 dynamic_slice.22
  55.6 75.7 %psum.14 = f32[3072]{0:T(1024)S(1)} all-reduce(f32[3072]{0:T(1024)S(1)} %and_select_fusion), channel_id=1, replica_groups=mesh['rows'=64,'feat'=8] {'feat'}, use_global_device_ids=true, to_apply=%region_4.5 | all-reduce | flops 3072 | bytes 24576 | tf_op jit(solution)/shard_map/psum | solution.py:110
  131.4 0.7 and_convert_fusion
  132.1 359.6 %reduce-scatter.2.cloned.1.call-done = f32[128,128]{1,0:T(8,128)} async-done(((f32[8192,128]{1,0:T(8,128)}), f32[128,128]{1,0:T(8,128)}) %reduce-scatter.2.cloned.1.call-update) | async-done | bytes 65552 | tf_op jit(solution)/shard_map/reduce_scatter | solution.py:70
  491.6 1.0 reshape.173
  493.5 110.9 %psum.15 = f32[8,2,64]{2,1,0:T(2,128)S(1)} all-reduce(f32[8,2,64]{2,1,0:T(2,128)S(1)} %broadcast_select_fusion.1), channel_id=1, replica_groups=mesh['rows'=64,'feat'=8] {'rows','feat'}, use_global_device_ids=true, to_apply=%region_11.12 | all-reduce | flops 1024 | bytes 8192 | tf_op jit(solution)/shard_map/psum | solution.py:129
  605.0 0.7 maximum_multiply_fusion
  605.6 1.1 fusion.5
  (55 shorter events, 4.3 us)
Async XLA Ops:
  7.2 484.5 %reduce-scatter.2.cloned.1.call-start = ((), (), s32[]{:S(2)}) async-start(), calls=%async_computation.1 | async-start | bytes 4259840 | tf_op jit(solution)/shard_map/reduce_scatter | solution.py:70
  51.6 0.7 copy-start.4
  51.6 1.9 copy-start.6
  51.6 2.5 copy-start.5
  51.6 3.7 copy-start.2
  51.6 3.9 copy-start.1
  51.6 554.0 %copy-start = (f32[3072,32]{0,1:T(8,128)S(1)}, f32[3072,32]{0,1:T(8,128)}, u32[]{:S(2)}) copy-start(f32[3072,32]{0,1:T(8,128)} %param.9) | copy-start | bytes 1179652
  604.5 2.2 copy-start.3
Sparse Core Ops, SparseCore 0:
  51.8 439.8 reduce-scatter.1
where the time goes:
time: 614 us
  waiting for transfers between devices  360 us (59%)
  blocking collectives  187 us (30%)
  local copies, waits for them, and re-layouts  26 us (4%)
  between operations  15.6 us (3%)
  matrix products  12.7 us (2%)
  other arithmetic  10.3 us (2%)
    reduce_scatter x1, waiting for transfers between devices, local(): lax.psum_scatter(product.reshape(lax.axis_size('rows') * own_rows, 2 * bi...  360 us
    psum x1, blocking collectives, local(): side_sums = lax.psum(placed, ('rows', 'feat'))  111 us
    psum x1, blocking collectives, local(): side_count = lax.psum(right_flag, 'feat')  75.7 us
  transfers between devices with their start and end apart: 1, of which 1 were waited for; matrix products, arithmetic and copies ran while one was open for 0% of the time, Pallas kernels for 0%

commit v1 on v0

--- a/solution.py
+++ b/solution.py
@@ -126,7 +126,7 @@
     placed = jnp.where(
         (node_iota == my_node)[:, None, None], entry[None], jnp.zeros((), jnp.float32)
     )
-    side_sums = lax.psum(placed, ("rows", "feat"))
+    side_sums = lax.psum(lax.psum(placed, "feat"), "rows")
     leaves = -side_sums[..., :classes] / (side_sums[..., classes:] + reg_lambda)
     update = jnp.dot(
         slot_hot.astype(jnp.float32),

time: 614 us -> 796 us (1.30)
  blocking collectives: 187 us -> 293 us
  waiting for transfers between devices: 360 us -> 435 us
    psum x2, blocking collectives: 187 us -> 293 us  [local(): side_sums = lax.psum(lax.psum(placed, 'feat'), 'rows')]
    reduce_scatter x1, waiting for transfers between devices: 360 us -> 435 us  [local(): lax.psum_scatter(product.reshape(lax.axis_size('rows') * own_rows, 2 * bi...]
where the time goes in v1:
time: 796 us
  waiting for transfers between devices  435 us (55%)
  blocking collectives  293 us (37%)
  local copies, waits for them, and re-layouts  26 us (3%)
  between operations  15.6 us (2%)
  matrix products  12.7 us (2%)
  other arithmetic  10.3 us (1%)
    reduce_scatter x1, waiting for transfers between devices, local(): lax.psum_scatter(product.reshape(lax.axis_size('rows') * own_rows, 2 * bi...  435 us
    psum x2, blocking collectives, local(): side_sums = lax.psum(lax.psum(placed, 'feat'), 'rows')  293 us
  transfers between devices with their start and end apart: 1, of which 1 were waited for; matrix products, arithmetic and copies ran while one was open for 0% of the time, Pallas kernels for 0%

profile of v1, /device:TPU:1, one launch (start us, length us, event | category | flops | bytes accessed | tf_op | source)
XLA Modules:
  0.0 795.7 jit_solution(3057478180173478022)
XLA Ops:
  7.2 1.1 exponential_reduce_fusion
  8.3 0.7 iota_compare_fusion.4
  9.0 1.1 subtract_convert_fusion
  10.2 25.2 %while.11 = (s32[]{:T(128)}, f32[4,512,512]{1,2,0:T(8,128)}, s32[4]{0:T(128)S(1)}, s32[3072,32]{0,1:T(8,128)}, bf16[3072,64]{0,1:T(8,128)(2,1)S(1)}, /*index=5*/...) while((s32[]{:T(128)}, f32[4,512,512]{1,2,0:T(8,128)}, ...), condition=%wide.region_7.8_spmd.clone, body=%wide.region_6.7_spmd.clone.sunk | while | flops 1613758464 | bytes 11207331 | solution.py:67
  10.2 0.6 dynamic_slice.31
  11.5 0.9 constant_dynamic-slice_fusion.2
  12.4 0.9 bitcast_compare_fusion.2
  13.7 2.8 fusion.35
  17.7 0.9 constant_dynamic-slice_fusion.2
  18.7 0.9 bitcast_compare_fusion.2
  19.9 2.8 fusion.35
  22.8 0.6 dynamic_slice.31
  24.0 0.9 constant_dynamic-slice_fusion.2
  25.0 0.9 bitcast_compare_fusion.2
  26.3 2.8 fusion.35
  29.1 0.6 dynamic_slice.31
  30.3 0.9 constant_dynamic-slice_fusion.2
  31.3 0.9 bitcast_compare_fusion.2
  32.5 2.8 fusion.35
  35.4 5.4 copy.31
  40.8 5.5 reshape_reshape.3
  46.3 5.4 copy.32
  52.3 0.6 dynamic_slice.19
  53.5 0.6 dynamic_slice.21
  54.1 0.6 dynamic_slice.22
  55.4 0.7 and_convert_fusion
  56.3 435.1 %reduce-scatter.2.cloned.1.call-done = f32[128,128]{1,0:T(8,128)} async-done(((f32[8192,128]{1,0:T(8,128)}), f32[128,128]{1,0:T(8,128)}) %reduce-scatter.2.cloned.1.call-update) | async-done | bytes 65552 | tf_op jit(solution)/shard_map/reduce_scatter | solution.py:70
  491.4 1.0 reshape.173
  493.2 70.5 %all-reduce = (f32[8,2,64]{2,1,0:T(2,128)S(1)}, f32[3072]{0:T(1024)S(1)}) all-reduce(f32[8,2,64]{2,1,0:T(2,128)S(1)} %broadcast_select_fusion.1, f32[3072]{0:T(1024)S(1)} %and_select_fusion), channel_id=1, replica_groups=mesh['rows'=64,'feat'=8] {'feat'}, use_global_device_ids=true, to_apply=%region_11.12 | all-reduce | flops 4096 | bytes 32768 | tf_op jit(solution)/shard_map/psum | solution.py:129
  563.7 222.8 %psum.23 = f32[8,2,64]{2,1,0:T(2,128)S(1)} all-reduce(f32[8,2,64]{2,1,0:T(2,128)S(1)} %get-tuple-element.68), channel_id=1, replica_groups=mesh['rows'=64,'feat'=8] {'rows'}, use_global_device_ids=true, to_apply=%region_12.13 | all-reduce | flops 1024 | bytes 8192 | tf_op jit(solution)/shard_map/psum | solution.py:129
  787.1 0.7 maximum_multiply_fusion
  787.8 1.1 fusion.5
  (55 shorter events, 4.4 us)
Async XLA Ops:
  7.2 484.2 %reduce-scatter.2.cloned.1.call-start = ((), (), s32[]{:S(2)}) async-start(), calls=%async_computation.1 | async-start | bytes 4259840 | tf_op jit(solution)/shard_map/reduce_scatter | solution.py:70
  51.6 0.7 copy-start.4
  51.6 1.9 copy-start.6
  51.6 2.5 copy-start.5
  51.6 4.4 copy-start.2
  51.6 4.6 copy-start.1
  51.6 736.1 %copy-start = (f32[3072,32]{0,1:T(8,128)S(1)}, f32[3072,32]{0,1:T(8,128)}, u32[]{:S(2)}) copy-start(f32[3072,32]{0,1:T(8,128)} %param.9) | copy-start | bytes 1179652
  786.6 2.2 copy-start.3
Sparse Core Ops, SparseCore 0:
  51.8 439.5 reduce-scatter.1
